TPU v7x, 512 devices: a whole 4x8x8 slice. The times are simulated.
512 devices in a mesh: tm: 32 (over x, z), space: 16 (over y, core).
Axes of the slice: x: 4, y: 8, z: 8, core: 2. Of those that a mesh axis runs over, the one named last changes fastest.
Arguments:
- inverse_factor: bfloat16 [32, 2048, 2048], P('tm', None, 'space'), as said below
- arrow_factor: bfloat16 [32, 64, 2048], P('tm', None, 'space'), may hold values from -6 to 6
- decay: float32 [32, 2048], P('tm'), may hold values from 0 to 1
- tip_inverse: float32 [64, 64], replicated, may hold values from -0.75 to 0.75
- sigma_end: float32 [2048, 2048], P(None, 'space'), may hold values from -2.7 to 2.7, as said below
- arrow_end: float32 [2048, 64], P('space'), may hold values from -6 to 6
Outputs:
- sigmas: float32 [32, 2048, 2048], P('tm', None, 'space')
- arrows: float32 [32, 2048, 64], P('tm', 'space')
Inputs may be any that keep to these rules, and one draw needn't show every extreme that they name: `inverse_factor`: each K_t is lower triangular with a positive diagonal. `sigma_end`: symmetric.
All inputs are finite; a program needn't handle non-finite values.
Results may differ from a plain program's by a relative error of at most 0.0003.
Values may be sent and summed in bfloat16 or wider, within the bound.
No kernel may reach another device: no remote copies, remote signals or barrier semaphores. Data moves between devices by JAX's collectives and lax.ppermute only.
A program may use at most 128 MiB of HBM per device.

v0:
```python
import jax
import jax.numpy as jnp
from jax import lax
from jax.sharding import PartitionSpec as P


def prefix(array, axis, combine, identity):
    devices, position = (lax.axis_size(axis), lax.axis_index(axis))
    everything = jax.tree.map(lambda part: lax.all_gather(part, axis), array)
    start = jax.tree.map(
        lambda part, zero: jnp.broadcast_to(jnp.asarray(zero, part.dtype), part.shape),
        array,
        identity,
    )

    def hop(k, before):
        at = devices - 1 - k
        reached = at > position
        new = combine(before, jax.tree.map(lambda part: part[at], everything))
        return jax.tree.map(lambda a, b: jnp.where(reached, a, b), new, before)

    return lax.fori_loop(0, devices, hop, start)


def column_products(left, right):
    return lax.dot_general(
        left, right, (((0,), (0,)), ((), ())), preferred_element_type=jnp.float32
    )


def compose(earlier, later):
    falloff_later, own_after, sigma_after, arrow_after = earlier
    lower_factor_current, own_here, sigma_here, border_column_current = later
    return (
        lower_factor_current * falloff_later,
        own_here * own_after,
        sigma_here + lower_factor_current[:, None] * own_here[None, :] * sigma_after,
        border_column_current + own_here[:, None] * arrow_after,
    )


def body(inverse_factor, arrow_factor, decay, tip_inverse, sigma_end, arrow_end):
    highest = lax.Precision.HIGHEST
    factor_cols = inverse_factor[0]
    order = factor_cols.shape[0]
    width = factor_cols.shape[1]
    panel_index = lax.axis_index("space")
    precision_panel = column_products(
        lax.all_gather(factor_cols, "space", axis=1, tiled=True), factor_cols
    )
    decay_all = decay[0]
    self_falloff = lax.dynamic_slice_in_dim(decay_all, panel_index * width, width)
    arrow_local = arrow_factor[0]
    arrow_wide = arrow_local.astype(jnp.float32)
    cross = lax.psum_scatter(
        lax.dot_general(
            precision_panel,
            arrow_wide,
            (((1,), (1,)), ((), ())),
            precision=highest,
            preferred_element_type=jnp.float32,
        ),
        "space",
        scatter_dimension=0,
        tiled=True,
    )
    own_arrow = -jnp.dot(cross, tip_inverse, precision=highest)
    arrow_cols_count = tip_inverse.shape[0]
    identity_matrix = (
        jnp.ones((order,), jnp.float32),
        jnp.ones((width,), jnp.float32),
        jnp.zeros((order, width), jnp.float32),
        jnp.zeros((width, arrow_cols_count), jnp.float32),
    )
    mine = (decay_all, self_falloff, precision_panel, own_arrow)
    later_decay, later_own, later_sigma, later_arrow = prefix(mine, "tm", compose, identity_matrix)
    covariance_following = later_sigma + later_decay[:, None] * later_own[None, :] * sigma_end
    spike_ahead = later_arrow + later_own[:, None] * arrow_end
    sigma_block = (
        precision_panel + decay_all[:, None] * self_falloff[None, :] * covariance_following
    )
    arrow_block = own_arrow + self_falloff[:, None] * spike_ahead
    return (sigma_block[None], arrow_block[None])


def solution(mesh):
    placed = (
        P("tm", None, "space"),
        P("tm", None, "space"),
        P("tm", None),
        P(),
        P(None, "space"),
        P("space", None),
    )
    return jax.shard_map(
        body,
        mesh=mesh,
        in_specs=placed,
        out_specs=(P("tm", None, "space"), P("tm", "space", None)),
        check_vma=False,
    )
```

profile of v0, /device:TPU:1, one launch (start us, length us, event | category | flops | bytes accessed | tf_op | source)
XLA Modules:
  0.0 611.4 jit_solution(3542080441122480926)
XLA Ops:
  8.0 76.7 %all-gather.9.cloned.1.call-done = bf16[1,2048,2048]{2,1,0:T(8,128)(2,1)} async-done(((bf16[1,2048,128]{2,1,0:T(8,128)(2,1)}), bf16[1,2048,2048]{2,1,0:T(8,128)(2,1)}) %all-gather.9.cloned.1.call-update) | async-done | bytes 8388624 | tf_op jit(solution)/shard_map/all_gather | solution.py:49
  84.7 5.8 fusion.3
  92.2 54.2 %reduce-scatter.2.cloned.1.call-done = f32[128,64]{1,0:T(8,128)} async-done(((f32[2048,64]{1,0:T(8,128)}), f32[128,64]{1,0:T(8,128)}) %reduce-scatter.2.cloned.1.call-update) | async-done | bytes 32784 | tf_op jit(solution)/shard_map/reduce_scatter | solution.py:55
  148.8 37.9 %all-gather.3 = f32[32,1,2048]{2,1,0:T(1,128)S(1)} all-gather(f32[1,1,2048]{2,1,0:T(1,128)S(1)} %bitcast.51), channel_id=1, replica_groups=mesh['tm'=32,'space'=16] {'tm'}, dimensions={0}, use_global_device_ids=true | all-gather | bytes 270336 | tf_op jit(solution)/shard_map/all_gather | solution.py:9
  187.4 33.0 %all-gather.4 = f32[32,1,128]{2,1,0:T(1,128)} all-gather(f32[1,1,128]{2,1,0:T(1,128)S(1)} %get-tuple-element.327), channel_id=1, replica_groups=mesh['tm'=32,'space'=16] {'tm'}, dimensions={0}, use_global_device_ids=true | all-gather | bytes 16896 | tf_op jit(solution)/shard_map/all_gather | solution.py:9
  220.4 4.0 all-gather.13.cloned.1.call-done
  224.4 3.1 copy.12
  227.5 243.0 %all-gather.11.cloned.1.call-done = f32[65536,128]{1,0:T(8,128)} async-done(((f32[2048,128]{1,0:T(8,128)}), f32[65536,128]{1,0:T(8,128)}) %all-gather.11.cloned.1.call-update) | async-done | bytes 33554448 | tf_op jit(solution)/shard_map/all_gather | solution.py:9
  470.5 130.7 %while.22 = (s32[]{:T(128)}, f32[2048]{0:T(1024)S(1)}, f32[128]{0:T(128)}, f32[2048,128]{1,0:T(8,128)S(1)}, f32[128,64]{1,0:T(8,128)S(1)}, /*index=5*/s32[]{:T(1...) while((s32[]{:T(128)}, f32[2048]{0:T(1024)S(1)}, ...), condition=%wide.region_2.3_spmd.clone, body=%wide.region_1.2_spmd.clone.sunk | while | flops 1350024 | bytes 3296485 | solution.py:22
  472.9 1.8 fusion.16
  477.0 1.8 fusion.16
  481.1 1.8 fusion.16
  485.2 1.8 fusion.16
  489.3 1.8 fusion.16
  493.3 1.8 fusion.16
  497.4 1.8 fusion.16
  501.5 1.8 fusion.16
  505.6 1.8 fusion.16
  509.7 1.8 fusion.16
  513.8 1.8 fusion.16
  517.8 1.8 fusion.16
  521.9 1.8 fusion.16
  526.0 1.8 fusion.16
  602.7 2.2 add_bitcast_fusion
  (178 shorter events, 111.0 us)
Async XLA Ops:
  7.2 139.2 %copy-start = (f32[64,64]{1,0:T(8,128)S(1)}, f32[64,64]{1,0:T(8,128)}, u32[]{:S(2)}) copy-start(f32[64,64]{1,0:T(8,128)} %param.11) | copy-start | bytes 49156
  7.2 83.3 %copy-start.6 = (bf16[1,64,128]{2,1,0:T(8,128)(2,1)S(1)}, bf16[1,64,128]{2,1,0:T(8,128)(2,1)}, u32[]{:S(2)}) copy-start(bf16[1,64,128]{2,1,0:T(8,128)(2,1)} %param.9) | copy-start | bytes 49156
  7.2 77.5 %all-gather.9.cloned.1.call-start = ((), (), s32[]{:S(2)}) async-start(), calls=%async_computation.2 | async-start | bytes 8912896 | tf_op jit(solution)/shard_map/all_gather | solution.py:49
  7.9 140.9 %copy-start.5 = (f32[1,2048]{1,0:T(1,128)S(1)}, f32[1,2048]{1,0:T(1,128)}, u32[]{:S(2)}) copy-start(f32[1,2048]{1,0:T(1,128)} %param.10) | copy-start | bytes 24580
  7.9 138.5 %reduce-scatter.2.cloned.1.call-start = ((), (), s32[]{:S(2)}) async-start(), calls=%async_computation.1 | async-start | bytes 1114112 | tf_op jit(solution)/shard_map/reduce_scatter | solution.py:55
  90.5 57.7 %copy-start.1 = (f32[2048,128]{1,0:T(8,128)}, f32[2048,128]{1,0:T(8,128)S(1)}, u32[]{:S(2)}) copy-start(f32[2048,128]{1,0:T(8,128)S(1)} %fusion.3) | copy-start | bytes 3145732
  92.1 132.3 %all-gather.13.cloned.1.call-start = ((), (), s32[]{:S(2)}) async-start(), calls=%async_computation.4 | async-start | bytes 1081344 | tf_op jit(solution)/shard_map/all_gather | solution.py:9
  148.1 322.3 %all-gather.11.cloned.1.call-start = ((), (), s32[]{:S(2)}) async-start(), calls=%async_computation.3 | async-start | bytes 34603008 | tf_op jit(solution)/shard_map/all_gather | solution.py:9
  470.5 130.8 %copy-start.4 = (f32[128,64]{0,1:T(8,128)S(1)}, f32[128,64]{0,1:T(8,128)}, u32[]{:S(2)}) copy-start(f32[128,64]{0,1:T(8,128)} %convolution_negate_fusion) | copy-start | bytes 98308
  470.5 132.2 %copy-start.2 = (f32[2048,128]{1,0:T(8,128)S(1)}, f32[2048,128]{1,0:T(8,128)}, u32[]{:S(2)}) copy-start(f32[2048,128]{1,0:T(8,128)} %copy-done.1) | copy-start | bytes 3145732
  470.5 132.2 %copy-start.3 = (f32[2048,128]{1,0:T(8,128)S(1)}, f32[2048,128]{1,0:T(8,128)}, u32[]{:S(2)}) copy-start(f32[2048,128]{1,0:T(8,128)} %param.12) | copy-start | bytes 3145732
Sparse Core Ops, SparseCore 0:
  10.1 74.5 all-gather.8
  92.2 54.1 reduce-scatter.1
  150.5 73.8 all-gather.12
  228.5 241.9 all-gather.10
where the time goes:
time: 615 us; the launch traced here: 611 us
  waiting for transfers between devices  379 us (62%)
  other arithmetic  132 us (21%)
  blocking collectives  70.9 us (12%)
  between operations  13.9 us (2%)
  matrix products  9.12 us (1%)
    all_gather x2, waiting for transfers between devices, prefix(): everything = jax.tree.map(lambda part: lax.all_gather(part, axis), array)  247 us
    select_n x128, other arithmetic, hop(): return jax.tree.map(lambda a, b: jnp.where(reached, a, b), new, before)  129 us
    all_gather x1, waiting for transfers between devices, body(): lax.all_gather(factor_cols, 'space', axis=1, tiled=True)  76.7 us
    all_gather x2, blocking collectives, prefix(): everything = jax.tree.map(lambda part: lax.all_gather(part, axis), array)  70.9 us
    reduce_scatter x1, waiting for transfers between devices, body(): lax.psum_scatter(lax.dot_general(precision_panel, arrow_wide, (((1,), (1,...  54.2 us
  transfers between devices with their start and end apart: 4, of which 4 were waited for; matrix products, arithmetic and copies ran while one was open for 1% of the time, Pallas kernels for 0%

commit v1 on v0

--- a/solution.py
+++ b/solution.py
@@ -2,6 +2,33 @@
 import jax.numpy as jnp
 from jax import lax
 from jax.sharding import PartitionSpec as P
+from jax.lax import axis_index, axis_size, ppermute
+
+
+def extend_desk_here(vals, ndim_at):
+    vals = jnp.moveaxis(vals, 0, ndim_at)
+    z = vals.shape
+    left_arr = vals.reshape(*z[:ndim_at], z[ndim_at] * z[ndim_at + 1], *z[ndim_at + 2 :])
+    return left_arr
+
+
+def pack_meshes(patch, along_axis, array_axis):
+    p_count = axis_size(along_axis)
+    buffers = list(map(lambda ii: (ii, (ii + 1) % p_count), range(p_count)))
+    arrivals = [(i, p) for p, i in buffers]
+    mid_arr, block_last = ([], [])
+    for jj in range(p_count - 1):
+        if jj % 2 == 0:
+            mid_arr.append(ppermute(mid_arr[-1] if mid_arr else patch, along_axis, buffers))
+        else:
+            block_last.append(
+                ppermute(block_last[-1] if block_last else patch, along_axis, arrivals)
+            )
+    back = jnp.stack([*mid_arr[::-1], patch, *block_last], axis=0)
+    f_next = axis_index(along_axis) - len(mid_arr)
+    back = back[(jnp.arange(p_count) - f_next) % p_count]
+    state_now = extend_desk_here(back, array_axis)
+    return state_now
 
 
 def prefix(array, axis, combine, identity):
@@ -45,9 +72,7 @@
     order = factor_cols.shape[0]
     width = factor_cols.shape[1]
     panel_index = lax.axis_index("space")
-    precision_panel = column_products(
-        lax.all_gather(factor_cols, "space", axis=1, tiled=True), factor_cols
-    )
+    precision_panel = column_products(pack_meshes(factor_cols, "space", 1), factor_cols)
     decay_all = decay[0]
     self_falloff = lax.dynamic_slice_in_dim(decay_all, panel_index * width, width)
     arrow_local = arrow_factor[0]

time: 615 us -> 665 us (1.081)
  starting transfers between devices: 0.16 us -> 60.3 us
  waiting for transfers between devices: 379 us -> 328 us
  local copies, waits for them, and re-layouts: 4.25 us -> 47 us
    all_gather x1 -> x0, waiting for transfers between devices: 76.7 us -> none  [body(): lax.all_gather(factor_cols, 'space', axis=1, tiled=True)]
    ppermute x0 -> x15, starting transfers between devices: none -> 60.2 us  [the longest x7 52.7 us: pack_meshes(): ppermute(block_last[-1] if block_last else patch, along_axis, arrivals)]
    unnamed x16 -> x47, local copies, waits for them, and re-layouts: 3.28 us -> 24.7 us
    ppermute x0 -> x15, waiting for transfers between devices: none -> 16 us  [the longest x8 10.9 us: pack_meshes(): ppermute(mid_arr[-1] if mid_arr else patch, along_axis, buffers)]
    transpose x0 -> x1, local copies, waits for them, and re-layouts: none -> 12.3 us  [extend_desk_here(): vals = jnp.moveaxis(vals, 0, ndim_at)]
    reduce_scatter x1, waiting for transfers between devices: 54.2 us -> 64 us  [body(): lax.psum_scatter(lax.dot_general(precision_panel, arrow_wide, (((1,), (1,...]
    gather x0 -> x1, local copies, waits for them, and re-layouts: none -> 8.17 us  [pack_meshes(): back = back[(jnp.arange(p_count) - f_next) % p_count]]
  transfers between devices with their start and end apart: 4 -> 18, of which waited for: 4 -> 14; matrix products, arithmetic and copies ran while one was open for 1% -> 4% of each run, Pallas kernels for 0% -> 0%
where the time goes in v1:
time: 665 us; the launch traced here: 660 us
  waiting for transfers between devices  328 us (49%)
  other arithmetic  130 us (20%)
  blocking collectives  70.9 us (11%)
  starting transfers between devices  60.3 us (9%)
  local copies, waits for them, and re-layouts  47 us (7%)
  between operations  13.9 us (2%)
  matrix products  8.89 us (1%)
    all_gather x2, waiting for transfers between devices, prefix(): everything = jax.tree.map(lambda part: lax.all_gather(part, axis), array)  247 us
    select_n x128, other arithmetic, hop(): return jax.tree.map(lambda a, b: jnp.where(reached, a, b), new, before)  126 us
    all_gather x2, blocking collectives, prefix(): everything = jax.tree.map(lambda part: lax.all_gather(part, axis), array)  70.9 us
    reduce_scatter x1, waiting for transfers between devices, body(): lax.psum_scatter(lax.dot_general(precision_panel, arrow_wide, (((1,), (1,...  64 us
    ppermute x7, starting transfers between devices, pack_meshes(): ppermute(block_last[-1] if block_last else patch, along_axis, arrivals)  52.7 us
    unnamed x47, local copies, waits for them, and re-layouts  24.7 us
  transfers between devices with their start and end apart: 18, of which 14 were waited for; matrix products, arithmetic and copies ran while one was open for 4% of the time, Pallas kernels for 0%

profile of v1, /device:TPU:1, one launch (start us, length us, event | category | flops | bytes accessed | tf_op | source)
XLA Modules:
  0.0 660.3 jit_solution(1558700467834395332)
XLA Ops:
  7.2 2.7 collective-permute-start
  9.9 6.4 collective-permute-done
  16.4 2.4 collective-permute-start.1
  18.8 5.4 collective-permute-start.8
  27.6 6.6 collective-permute-start.9
  36.2 7.7 %collective-permute-start.10 = (bf16[2048,128]{1,0:T(8,128)(2,1)S(1)}, bf16[2048,128]{1,0:T(8,128)(2,1)S(1)}, u32[]{:S(2)}, u32[]{:S(2)}) collective-permute-start(bf16[2048,128]{1,0:T(8,128)(2,1)S(1)} %collective-permute-done.9), channel_id=1, source_target_pairs={{1,0},{2,1},{3,2},{4,3},{5,4},{6,5},{7,6},{8,7},{9,8},{10,9},{11,1... | collective-permute-start | bytes 1572872 | tf_op jit(solution)/shard_map/ppermute | solution.py:25
  46.2 8.3 %collective-permute-start.11 = (bf16[2048,128]{1,0:T(8,128)(2,1)S(1)}, bf16[2048,128]{1,0:T(8,128)(2,1)S(1)}, u32[]{:S(2)}, u32[]{:S(2)}) collective-permute-start(bf16[2048,128]{1,0:T(8,128)(2,1)S(1)} %collective-permute-done.10), channel_id=1, source_target_pairs={{1,0},{2,1},{3,2},{4,3},{5,4},{6,5},{7,6},{8,7},{9,8},{10,9},{11,1... | collective-permute-start | bytes 1572872 | tf_op jit(solution)/shard_map/ppermute | solution.py:25
  56.8 8.2 %collective-permute-start.12 = (bf16[2048,128]{1,0:T(8,128)(2,1)S(1)}, bf16[2048,128]{1,0:T(8,128)(2,1)}, u32[]{:S(2)}, u32[]{:S(2)}) collective-permute-start(bf16[2048,128]{1,0:T(8,128)(2,1)S(1)} %collective-permute-done.11), channel_id=1, source_target_pairs={{1,0},{2,1},{3,2},{4,3},{5,4},{6,5},{7,6},{8,7},{9,8},{10,9},{11,1... | collective-permute-start | bytes 1572872 | tf_op jit(solution)/shard_map/ppermute | solution.py:25
  66.7 8.1 %collective-permute-start.13 = (bf16[2048,128]{1,0:T(8,128)(2,1)}, bf16[2048,128]{1,0:T(8,128)(2,1)}, u32[]{:S(2)}, u32[]{:S(2)}) collective-permute-start(bf16[2048,128]{1,0:T(8,128)(2,1)} %collective-permute-done.12), channel_id=1, source_target_pairs={{1,0},{2,1},{3,2},{4,3},{5,4},{6,5},{7,6},{8,7},{9,8},{10,9},{11,1... | collective-permute-start | bytes 1572872 | tf_op jit(solution)/shard_map/ppermute | solution.py:25
  76.8 8.4 %collective-permute-start.14 = (bf16[2048,128]{1,0:T(8,128)(2,1)}, bf16[2048,128]{1,0:T(8,128)(2,1)S(1)}, u32[]{:S(2)}, u32[]{:S(2)}) collective-permute-start(bf16[2048,128]{1,0:T(8,128)(2,1)} %collective-permute-done.13), channel_id=1, source_target_pairs={{1,0},{2,1},{3,2},{4,3},{5,4},{6,5},{7,6},{8,7},{9,8},{10,9},{11,1... | collective-permute-start | bytes 1572872 | tf_op jit(solution)/shard_map/ppermute | solution.py:25
  87.0 1.9 bitcast_dynamic-update-slice_fusion.13
  92.6 1.9 bitcast_dynamic-update-slice_fusion.10
  103.0 1.9 bitcast_dynamic-update-slice_fusion.1
  105.8 8.2 %gather_fusion = bf16[16,2048,128]{2,1,0:T(8,128)(2,1)} fusion(bf16[16,2048,128]{2,1,0:T(8,128)(2,1)} %bitcast_dynamic-update-slice_fusion, s32[1024]{0:T(1024)S(1)} %pad_clamp_fusion), kind=kCustom, calls=%fused_computation | custom fusion | bytes 16777280 | tf_op jit(solution)/shard_map/gather | solution.py:29
  114.0 12.3 %copy.15 = bf16[2048,16,128]{0,2,1:T(8,128)(2,1)} copy(bf16[2048,16,128]{2,0,1:T(8,128)(2,1)} %bitcast.78) | data formatting | bytes 16777216 | tf_op jit(solution)/shard_map/transpose | solution.py:9
  126.3 5.7 fusion.9
  133.7 64.0 %reduce-scatter.2.cloned.1.call-done = f32[128,64]{0,1:T(8,128)} async-done(((f32[2048,64]{0,1:T(8,128)}), f32[128,64]{0,1:T(8,128)}) %reduce-scatter.2.cloned.1.call-update) | async-done | bytes 32784 | tf_op jit(solution)/shard_map/reduce_scatter | solution.py:80
  200.2 37.8 %all-gather.2 = f32[32,1,2048]{2,1,0:T(1,128)S(1)} all-gather(f32[1,1,2048]{2,1,0:T(1,128)S(1)} %bitcast.87), channel_id=1, replica_groups=mesh['tm'=32,'space'=16] {'tm'}, dimensions={0}, use_global_device_ids=true | all-gather | bytes 270336 | tf_op jit(solution)/shard_map/all_gather | solution.py:36
  238.7 33.1 %all-gather.3 = f32[32,1,128]{2,1,0:T(1,128)} all-gather(f32[1,1,128]{2,1,0:T(1,128)S(1)} %get-tuple-element.347), channel_id=1, replica_groups=mesh['tm'=32,'space'=16] {'tm'}, dimensions={0}, use_global_device_ids=true | all-gather | bytes 16896 | tf_op jit(solution)/shard_map/all_gather | solution.py:36
  271.7 4.0 all-gather.9.cloned.1.call-done
  275.7 3.2 copy.18
  278.9 243.1 %all-gather.7.cloned.1.call-done = f32[65536,128]{1,0:T(8,128)} async-done(((f32[2048,128]{1,0:T(8,128)}), f32[65536,128]{1,0:T(8,128)}) %all-gather.7.cloned.1.call-update) | async-done | bytes 33554448 | tf_op jit(solution)/shard_map/all_gather | solution.py:36
  522.0 128.1 %while.22 = (s32[]{:T(128)}, f32[2048]{0:T(1024)S(1)}, f32[128]{0:T(128)}, f32[2048,128]{1,0:T(8,128)S(1)}, f32[128,64]{1,0:T(8,128)S(1)}, /*index=5*/s32[]{:T(1...) while((s32[]{:T(128)}, f32[2048]{0:T(1024)S(1)}, ...), condition=%wide.region_2.3_spmd.clone, body=%wide.region_1.2_spmd.clone.sunk | while | flops 1350024 | bytes 3296485 | solution.py:49
  651.6 2.2 add_bitcast_fusion
  (241 shorter events, 161.3 us)
Async XLA Ops:
  7.2 190.6 %copy-start = (f32[64,64]{1,0:T(8,128)S(1)}, f32[64,64]{1,0:T(8,128)}, u32[]{:S(2)}) copy-start(f32[64,64]{1,0:T(8,128)} %param.11) | copy-start | bytes 49156
  7.2 89.8 %copy-start.4 = (bf16[1,2048,128]{2,1,0:T(8,128)(2,1)S(1)}, bf16[1,2048,128]{2,1,0:T(8,128)(2,1)}, u32[]{:S(2)}) copy-start(bf16[1,2048,128]{2,1,0:T(8,128)(2,1)} %param.8) | copy-start | bytes 1572868
  7.2 190.6 %reduce-scatter.2.cloned.1.call-start = ((), (), s32[]{:S(2)}) async-start(), calls=%async_computation.1 | async-start | bytes 557056 | tf_op jit(solution)/shard_map/reduce_scatter | solution.py:80
  7.2 9.1 %collective-permute-start = (bf16[2048,128]{1,0:T(8,128)(2,1)}, bf16[2048,128]{1,0:T(8,128)(2,1)S(1)}, u32[]{:S(2)}, u32[]{:S(2)}) collective-permute-start(bf16[2048,128]{1,0:T(8,128)(2,1)} %bitcast.84), channel_id=1, source_target_pairs={{0,1},{1,2},{2,3},{3,4},{4,5},{5,6},{6,7},{7,8},{8,9},{9,10},{10,1... | collective-permute-start | bytes 1572872 | tf_op jit(solution)/shard_map/ppermute | solution.py:22
  16.4 9.2 %collective-permute-start.1 = (bf16[2048,128]{1,0:T(8,128)(2,1)S(1)}, bf16[2048,128]{1,0:T(8,128)(2,1)S(1)}, u32[]{:S(2)}, u32[]{:S(2)}) collective-permute-start(bf16[2048,128]{1,0:T(8,128)(2,1)S(1)} %collective-permute-done), channel_id=1, source_target_pairs={{0,1},{1,2},{2,3},{3,4},{4,5},{5,6},{6,7},{7,8},{8,9},{9,10},{10,1... | collective-permute-start | bytes 1572872 | tf_op jit(solution)/shard_map/ppermute | solution.py:22
  18.8 8.8 %collective-permute-start.8 = (bf16[2048,128]{1,0:T(8,128)(2,1)}, bf16[2048,128]{1,0:T(8,128)(2,1)S(1)}, u32[]{:S(2)}, u32[]{:S(2)}) collective-permute-start(bf16[2048,128]{1,0:T(8,128)(2,1)} %bitcast.85), channel_id=1, source_target_pairs={{1,0},{2,1},{3,2},{4,3},{5,4},{6,5},{7,6},{8,7},{9,8},{10,9},{11,1... | collective-permute-start | bytes 1572872 | tf_op jit(solution)/shard_map/ppermute | solution.py:25
  25.6 9.8 %collective-permute-start.2 = (bf16[2048,128]{1,0:T(8,128)(2,1)S(1)}, bf16[2048,128]{1,0:T(8,128)(2,1)S(1)}, u32[]{:S(2)}, u32[]{:S(2)}) collective-permute-start(bf16[2048,128]{1,0:T(8,128)(2,1)S(1)} %collective-permute-done.1), channel_id=1, source_target_pairs={{0,1},{1,2},{2,3},{3,4},{4,5},{5,6},{6,7},{7,8},{8,9},{9,10},{10,1... | collective-permute-start | bytes 1572872 | tf_op jit(solution)/shard_map/ppermute | solution.py:22
  27.6 8.6 %collective-permute-start.9 = (bf16[2048,128]{1,0:T(8,128)(2,1)S(1)}, bf16[2048,128]{1,0:T(8,128)(2,1)S(1)}, u32[]{:S(2)}, u32[]{:S(2)}) collective-permute-start(bf16[2048,128]{1,0:T(8,128)(2,1)S(1)} %collective-permute-done.8), channel_id=1, source_target_pairs={{1,0},{2,1},{3,2},{4,3},{5,4},{6,5},{7,6},{8,7},{9,8},{10,9},{11,1... | collective-permute-start | bytes 1572872 | tf_op jit(solution)/shard_map/ppermute | solution.py:25
  35.4 9.8 %collective-permute-start.3 = (bf16[2048,128]{1,0:T(8,128)(2,1)S(1)}, bf16[2048,128]{1,0:T(8,128)(2,1)S(1)}, u32[]{:S(2)}, u32[]{:S(2)}) collective-permute-start(bf16[2048,128]{1,0:T(8,128)(2,1)S(1)} %collective-permute-done.2), channel_id=1, source_target_pairs={{0,1},{1,2},{2,3},{3,4},{4,5},{5,6},{6,7},{7,8},{8,9},{9,10},{10,1... | collective-permute-start | bytes 1572872 | tf_op jit(solution)/shard_map/ppermute | solution.py:22
  36.2 9.2 %collective-permute-start.10 = (bf16[2048,128]{1,0:T(8,128)(2,1)S(1)}, bf16[2048,128]{1,0:T(8,128)(2,1)S(1)}, u32[]{:S(2)}, u32[]{:S(2)}) collective-permute-start(bf16[2048,128]{1,0:T(8,128)(2,1)S(1)} %collective-permute-done.9), channel_id=1, source_target_pairs={{1,0},{2,1},{3,2},{4,3},{5,4},{6,5},{7,6},{8,7},{9,8},{10,9},{11,1... | collective-permute-start | bytes 1572872 | tf_op jit(solution)/shard_map/ppermute | solution.py:25
  45.2 9.8 %collective-permute-start.4 = (bf16[2048,128]{1,0:T(8,128)(2,1)S(1)}, bf16[2048,128]{1,0:T(8,128)(2,1)S(1)}, u32[]{:S(2)}, u32[]{:S(2)}) collective-permute-start(bf16[2048,128]{1,0:T(8,128)(2,1)S(1)} %collective-permute-done.3), channel_id=1, source_target_pairs={{0,1},{1,2},{2,3},{3,4},{4,5},{5,6},{6,7},{7,8},{8,9},{9,10},{10,1... | collective-permute-start | bytes 1572872 | tf_op jit(solution)/shard_map/ppermute | solution.py:22
  46.2 9.9 %collective-permute-start.11 = (bf16[2048,128]{1,0:T(8,128)(2,1)S(1)}, bf16[2048,128]{1,0:T(8,128)(2,1)S(1)}, u32[]{:S(2)}, u32[]{:S(2)}) collective-permute-start(bf16[2048,128]{1,0:T(8,128)(2,1)S(1)} %collective-permute-done.10), channel_id=1, source_target_pairs={{1,0},{2,1},{3,2},{4,3},{5,4},{6,5},{7,6},{8,7},{9,8},{10,9},{11,1... | collective-permute-start | bytes 1572872 | tf_op jit(solution)/shard_map/ppermute | solution.py:25
  55.0 10.1 %collective-permute-start.5 = (bf16[2048,128]{1,0:T(8,128)(2,1)S(1)}, bf16[2048,128]{1,0:T(8,128)(2,1)S(1)}, u32[]{:S(2)}, u32[]{:S(2)}) collective-permute-start(bf16[2048,128]{1,0:T(8,128)(2,1)S(1)} %collective-permute-done.4), channel_id=1, source_target_pairs={{0,1},{1,2},{2,3},{3,4},{4,5},{5,6},{6,7},{7,8},{8,9},{9,10},{10,1... | collective-permute-start | bytes 1572872 | tf_op jit(solution)/shard_map/ppermute | solution.py:22
  56.8 9.9 %collective-permute-start.12 = (bf16[2048,128]{1,0:T(8,128)(2,1)S(1)}, bf16[2048,128]{1,0:T(8,128)(2,1)}, u32[]{:S(2)}, u32[]{:S(2)}) collective-permute-start(bf16[2048,128]{1,0:T(8,128)(2,1)S(1)} %collective-permute-done.11), channel_id=1, source_target_pairs={{1,0},{2,1},{3,2},{4,3},{5,4},{6,5},{7,6},{8,7},{9,8},{10,9},{11,1... | collective-permute-start | bytes 1572872 | tf_op jit(solution)/shard_map/ppermute | solution.py:25
  65.1 9.8 %collective-permute-start.6 = (bf16[2048,128]{1,0:T(8,128)(2,1)S(1)}, bf16[2048,128]{1,0:T(8,128)(2,1)}, u32[]{:S(2)}, u32[]{:S(2)}) collective-permute-start(bf16[2048,128]{1,0:T(8,128)(2,1)S(1)} %collective-permute-done.5), channel_id=1, source_target_pairs={{0,1},{1,2},{2,3},{3,4},{4,5},{5,6},{6,7},{7,8},{8,9},{9,10},{10,1... | collective-permute-start | bytes 1572872 | tf_op jit(solution)/shard_map/ppermute | solution.py:22
  66.7 10.0 %collective-permute-start.13 = (bf16[2048,128]{1,0:T(8,128)(2,1)}, bf16[2048,128]{1,0:T(8,128)(2,1)}, u32[]{:S(2)}, u32[]{:S(2)}) collective-permute-start(bf16[2048,128]{1,0:T(8,128)(2,1)} %collective-permute-done.12), channel_id=1, source_target_pairs={{1,0},{2,1},{3,2},{4,3},{5,4},{6,5},{7,6},{8,7},{9,8},{10,9},{11,1... | collective-permute-start | bytes 1572872 | tf_op jit(solution)/shard_map/ppermute | solution.py:25
  74.9 10.2 %collective-permute-start.7 = (bf16[2048,128]{1,0:T(8,128)(2,1)}, bf16[2048,128]{1,0:T(8,128)(2,1)}, u32[]{:S(2)}, u32[]{:S(2)}) collective-permute-start(bf16[2048,128]{1,0:T(8,128)(2,1)} %collective-permute-done.6), channel_id=1, source_target_pairs={{0,1},{1,2},{2,3},{3,4},{4,5},{5,6},{6,7},{7,8},{8,9},{9,10},{10,1... | collective-permute-start | bytes 1572872 | tf_op jit(solution)/shard_map/ppermute | solution.py:22
  76.8 28.2 %collective-permute-start.14 = (bf16[2048,128]{1,0:T(8,128)(2,1)}, bf16[2048,128]{1,0:T(8,128)(2,1)S(1)}, u32[]{:S(2)}, u32[]{:S(2)}) collective-permute-start(bf16[2048,128]{1,0:T(8,128)(2,1)} %collective-permute-done.13), channel_id=1, source_target_pairs={{1,0},{2,1},{3,2},{4,3},{5,4},{6,5},{7,6},{8,7},{9,8},{10,9},{11,1... | collective-permute-start | bytes 1572872 | tf_op jit(solution)/shard_map/ppermute | solution.py:25
  126.3 73.8 %copy-start.13 = (f32[1,2048]{1,0:T(1,128)S(1)}, f32[1,2048]{1,0:T(1,128)}, u32[]{:S(2)}) copy-start(f32[1,2048]{1,0:T(1,128)} %param.10) | copy-start | bytes 24580
  133.7 142.1 %all-gather.9.cloned.1.call-start = ((), (), s32[]{:S(2)}) async-start(), calls=%async_computation.3 | async-start | bytes 1081344 | tf_op jit(solution)/shard_map/all_gather | solution.py:36
  199.4 322.6 %all-gather.7.cloned.1.call-start = ((), (), s32[]{:S(2)}) async-start(), calls=%async_computation.2 | async-start | bytes 34603008 | tf_op jit(solution)/shard_map/all_gather | solution.py:36
  522.0 128.2 %copy-start.12 = (f32[128,64]{0,1:T(8,128)S(1)}, f32[128,64]{0,1:T(8,128)}, u32[]{:S(2)}) copy-start(f32[128,64]{0,1:T(8,128)} %convolution_negate_fusion) | copy-start | bytes 98308
  522.0 129.6 %copy-start.2 = (f32[2048,128]{1,0:T(8,128)S(1)}, f32[2048,128]{1,0:T(8,128)}, u32[]{:S(2)}) copy-start(f32[2048,128]{1,0:T(8,128)} %copy-done.1) | copy-start | bytes 3145732
  522.0 129.6 %copy-start.3 = (f32[2048,128]{1,0:T(8,128)S(1)}, f32[2048,128]{1,0:T(8,128)}, u32[]{:S(2)}) copy-start(f32[2048,128]{1,0:T(8,128)} %param.12) | copy-start | bytes 3145732
  (9 other events, 176.0 us)
Sparse Core Ops, SparseCore 0:
  133.8 63.9 reduce-scatter.1
  201.8 73.8 all-gather.8
  280.0 241.9 all-gather.6
